TPU v7x, 32 devices: a whole 2x2x4 slice. The times are simulated.
32 devices in a mesh: side: 2 (over core), dev: 16 (over z, y, x).
Axes of the slice: x: 2, y: 2, z: 4, core: 2. Of those that a mesh axis runs over, the one named last changes fastest.
Arguments:
- queries: bfloat16 [512, 4096], P(('side', 'dev')), may hold values from -150 to 150
- cached_key_table: bfloat16 [512, 256, 256], P(('side', 'dev')), may hold values from -6 to 6
- cached_value_table: bfloat16 [512, 256, 256], P(('side', 'dev')), may hold values from -12 to 12
- incoming_keys: bfloat16 [512, 256], P(('side', 'dev')), may hold values from -6 to 6
- incoming_values: bfloat16 [512, 256], P(('side', 'dev')), may hold values from -12 to 12
- context_length_per_row: int32 [512], P(('side', 'dev')), may hold values from 1 to 256, as said below
- residual: bfloat16 [512, 4096], P(('side', 'dev')), may hold values from -2 to 2
- norm_gain: bfloat16 [4096], replicated, may hold values from 0.099609375 to 1.8984375
- expert_ids: int32 [512, 8], P(('side', 'dev')), may hold values from 0 to 15, all different within a row; in each aligned block of 16 rows (0 to 15, 16 to 31, ...) at most 16 rows name the same one
- gate_weights: float32 [512, 8], P(('side', 'dev')), may hold values from 0.05 to 0.5
- gate_proj: bfloat16 [16, 4096, 1536], P('dev', None, 'side'), may hold values from -0.09375 to 0.09375
- up_proj: bfloat16 [16, 4096, 1536], P('dev', None, 'side'), may hold values from -0.09375 to 0.09375
- down_proj: bfloat16 [16, 1536, 4096], P('dev', 'side'), may hold values from -0.15625 to 0.15625
Outputs:
- layer_out: bfloat16 [512, 4096], P(('side', 'dev'))
Inputs may be any that keep to these rules, and one draw needn't show every extreme that they name: `context_length_per_row`: some row uses all 256 cached positions. `expert_ids`: each row names 8 different experts; among the rows of one device no expert is named more than 16 times, a bound that some block reaches.
All inputs are finite; a program needn't handle non-finite values.
Results may differ from a plain program's by a relative error of at most 0.011.
Values may be sent and summed in bfloat16 or wider, within the bound.
A program may use at most 128 MiB of HBM per device.

v0:
```python
import jax
import jax.numpy as jnp
from jax import lax
from jax.sharding import PartitionSpec as P

QUERY_HEADS = 32
KEY_VALUE_HEADS = 2
HEAD_SIZE = 128


def attend(
    queries,
    cached_key_table,
    cached_value_table,
    incoming_keys,
    incoming_values,
    context_length_per_row,
):
    count_of_rows, span_length, _ = cached_key_table.shape
    heads_of_queries = queries.reshape(
        count_of_rows, KEY_VALUE_HEADS, QUERY_HEADS // KEY_VALUE_HEADS, HEAD_SIZE
    )
    heads_of_keys = cached_key_table.reshape(count_of_rows, span_length, KEY_VALUE_HEADS, HEAD_SIZE)
    heads_of_values = cached_value_table.reshape(
        count_of_rows, span_length, KEY_VALUE_HEADS, HEAD_SIZE
    )
    newest_key = incoming_keys.reshape(count_of_rows, KEY_VALUE_HEADS, HEAD_SIZE)
    newest_value = incoming_values.reshape(count_of_rows, KEY_VALUE_HEADS, HEAD_SIZE)
    score_scale = HEAD_SIZE ** (-0.5)
    cached = (
        jnp.einsum(
            "rkgd,rlkd->rkgl", heads_of_queries, heads_of_keys, preferred_element_type=jnp.float32
        )
        * score_scale
    )
    fresh = (
        jnp.einsum(
            "rkgd,rkd->rkg", heads_of_queries, newest_key, preferred_element_type=jnp.float32
        )
        * score_scale
    )
    valid_mask = jnp.arange(span_length, dtype=jnp.int32)[None, :] < context_length_per_row[:, None]
    cached = jnp.where(valid_mask[:, None, None, :], cached, jnp.float32(-1e30))
    top_score = jnp.maximum(jnp.max(cached, axis=-1), fresh)
    exp_cached = jnp.exp(cached - top_score[..., None])
    exp_fresh = jnp.exp(fresh - top_score)
    denominator = jnp.sum(exp_cached, axis=-1) + exp_fresh
    prob_cached = (exp_cached / denominator[..., None]).astype(jnp.bfloat16)
    prob_fresh = (exp_fresh / denominator).astype(jnp.bfloat16)
    mixed = jnp.einsum(
        "rkgl,rlkd->rkgd", prob_cached, heads_of_values, preferred_element_type=jnp.float32
    )
    mixed = (
        mixed
        + prob_fresh.astype(jnp.float32)[..., None]
        * newest_value.astype(jnp.float32)[:, :, None, :]
    )
    return mixed.reshape(count_of_rows, QUERY_HEADS * HEAD_SIZE)


def placement(chosen_ids, expert_count, slot_cap):
    count_of_rows, top_count = chosen_ids.shape
    flat_ids = chosen_ids.reshape(count_of_rows * top_count)
    onehot = (flat_ids[:, None] == jnp.arange(expert_count, dtype=jnp.int32)[None, :]).astype(
        jnp.int32
    )
    before = jnp.cumsum(onehot, axis=0) - onehot
    slot_of = jnp.sum(before * onehot, axis=1)
    target = flat_ids * slot_cap + slot_of
    table = jnp.arange(expert_count * slot_cap, dtype=jnp.int32)[:, None] == target[None, :]
    return table.reshape(expert_count * slot_cap, count_of_rows, top_count)


def expert_act(slot_rows, gate_proj, up_proj):
    gate_val = jnp.dot(slot_rows, gate_proj[0], preferred_element_type=jnp.float32)
    up_val = jnp.dot(slot_rows, up_proj[0], preferred_element_type=jnp.float32)
    return (jax.nn.silu(gate_val) * up_val).astype(jnp.bfloat16)


def pack_rows(table, normed, expert_count, slot_cap):
    spread = jnp.sum(table, axis=2).astype(jnp.bfloat16)
    filled = jnp.dot(spread, normed, preferred_element_type=jnp.float32).astype(jnp.bfloat16)
    return filled.reshape(expert_count, slot_cap, normed.shape[1])


def on_device(
    queries,
    cached_key_table,
    cached_value_table,
    incoming_keys,
    incoming_values,
    context_length_per_row,
    residual,
    norm_gain,
    expert_ids,
    gate_weights,
    gate_proj,
    up_proj,
    down_proj,
):
    count_of_rows, width = residual.shape
    top_count = expert_ids.shape[1]
    expert_count = lax.axis_size("dev")
    slot_cap = min(count_of_rows, max(6, 2 * count_of_rows * top_count // expert_count))
    attn = attend(
        queries,
        cached_key_table,
        cached_value_table,
        incoming_keys,
        incoming_values,
        context_length_per_row,
    )
    hidden = (residual.astype(jnp.float32) + attn).astype(jnp.bfloat16)
    wide = hidden.astype(jnp.float32)
    mean_square = jnp.mean(wide * wide, axis=-1, keepdims=True)
    normed = (wide * lax.rsqrt(mean_square + 1e-06) * norm_gain.astype(jnp.float32)).astype(
        jnp.bfloat16
    )
    own_table = placement(expert_ids, expert_count, slot_cap)
    both_normed, both_ids = (
        lax.all_gather(normed, "side", axis=0, tiled=True),
        lax.all_gather(expert_ids, "side", axis=0, tiled=True),
    )
    first_block = pack_rows(
        placement(both_ids[:count_of_rows], expert_count, slot_cap),
        both_normed[:count_of_rows],
        expert_count,
        slot_cap,
    )
    second_block = pack_rows(
        placement(both_ids[count_of_rows:], expert_count, slot_cap),
        both_normed[count_of_rows:],
        expert_count,
        slot_cap,
    )
    outgoing = jnp.stack([first_block, second_block], axis=1)
    arrived = lax.all_to_all(outgoing, "dev", split_axis=0, concat_axis=0, tiled=True)
    act = expert_act(arrived.reshape(-1, width), gate_proj, up_proj)
    partial_value = jnp.dot(act, down_proj[0], preferred_element_type=jnp.float32)
    partial_value = partial_value.reshape(expert_count, 2, slot_cap, width)
    summed = lax.psum_scatter(partial_value, "side", scatter_dimension=1, tiled=True).reshape(
        expert_count, slot_cap, width
    )
    returned = lax.all_to_all(
        summed.astype(jnp.bfloat16), "dev", split_axis=0, concat_axis=0, tiled=True
    )
    combine = jnp.sum(own_table.astype(jnp.float32) * gate_weights[None, :, :], axis=2)
    moe_sum = jnp.dot(
        combine.T, returned.reshape(-1, width).astype(jnp.float32), precision=lax.Precision.HIGHEST
    )
    return (hidden.astype(jnp.float32) + moe_sum).astype(jnp.bfloat16)


def solution(mesh):
    in_specs = (
        P(("side", "dev"), None),
        P(("side", "dev"), None, None),
        P(("side", "dev"), None, None),
        P(("side", "dev"), None),
        P(("side", "dev"), None),
        P(("side", "dev")),
        P(("side", "dev"), None),
        P(),
        P(("side", "dev"), None),
        P(("side", "dev"), None),
        P("dev", None, "side"),
        P("dev", None, "side"),
        P("dev", "side", None),
    )
    out_specs = P(("side", "dev"), None)
    return jax.shard_map(
        on_device, mesh=mesh, in_specs=in_specs, out_specs=out_specs, check_vma=False
    )
```

profile of v0, /device:TPU:14, one launch (start us, length us, event | category | flops | bytes accessed | tf_op | source)
XLA Modules:
  0.0 228.3 jit_solution(14414867459490850878)
XLA Ops:
  0.0 1.1 copy.71
  1.1 0.7 iota_compare_fusion.6
  1.8 0.7 reshape.142
  2.5 0.2 fusion.44
  2.7 0.8 fusion.43
  3.5 0.3 fusion.25
  3.9 2.1 fusion.22
  6.0 0.3 fusion.26
  6.3 0.1 fusion.28
  6.4 2.0 all_gather.7
  8.4 1.8 all-gather
  10.2 0.1 copy.56
  10.3 0.1 eq.95
  10.3 0.1 fusion.35
  10.4 0.2 reduce_window_sum.24
  10.6 0.2 select_reduce_fusion.2
  10.8 0.1 reduce_sum.83
  10.9 0.1 copy.57
  11.0 0.1 eq.102
  11.1 0.1 fusion.34
  11.2 0.2 reduce_window_sum.25
  11.4 0.2 select_reduce_fusion.1
  11.6 0.1 reduce_sum.87
  11.7 0.1 copy.60
  11.7 0.1 copy.58
  11.8 0.1 convert_reduce_fusion.1
  12.0 0.1 convert_reduce_fusion
  12.1 0.7 convolution_convert_fusion.1
  12.9 0.7 convolution_convert_fusion
  13.6 2.3 %pad_maximum_fusion = bf16[16,2,16,4096]{3,2,1,0:T(8,128)(2,1)} fusion(bf16[16,1,16,4096]{3,2,1,0:T(8,128)(2,1)S(1)} %bitcast.77, bf16[16,1,16,4096]{3,2,1,0:T(8,128)(2,1)S(1)} %bitcast.76), kind=kLoop, calls=%fused_computation.10 | loop fusion | flops 2097152 | bytes 8388608 | tf_op jit(solution)/shard_map/stack | solution.py:136
  15.9 7.3 %all-to-all-start = ((bf16[16,2,16,4096]{3,2,1,0:T(8,128)(2,1)}), bf16[16,2,16,4096]{3,2,1,0:T(8,128)(2,1)}, u32[]{:S(2)}, u32[]{:S(2)}) async-start(bf16[16,2,16,4096]{3,2,1,0:T(8,128)(2,1)} %pad_maximum_fusion), calls=%async_computation | async-start | bytes 8388608 | tf_op jit(solution)/shard_map/all_to_all | solution.py:137
  23.2 0.6 dynamic-slice
  23.8 95.0 %all-to-all-done = bf16[16,2,16,4096]{3,2,1,0:T(8,128)(2,1)} async-done(((bf16[16,2,16,4096]{3,2,1,0:T(8,128)(2,1)}), bf16[16,2,16,4096]{3,2,1,0:T(8,128)(2,1)}, u32[]{:S(2)}, u32[]{:S(2)}) %all-to-all-start) | async-done | bytes 4194336 | tf_op jit(solution)/shard_map/all_to_all | solution.py:137
  118.9 7.0 %fusion.4 = f32[512,768]{1,0:T(8,128)S(1)} fusion(bf16[512,4096]{1,0:T(8,128)(2,1)} %bitcast.9, bf16[1,4096,768]{2,1,0:T(8,128)(2,1)} %param.23), kind=kOutput, calls=%fused_computation.4 | convolution fusion | flops 3221225472 | bytes 12058624 | tf_op jit(solution)/shard_map/dot_general | solution.py:75
  125.9 7.6 %multiply_convert_fusion = bf16[512,768]{1,0:T(8,128)(2,1)S(1)} fusion(f32[512,768]{1,0:T(8,128)S(1)} %fusion.4, bf16[512,4096]{1,0:T(8,128)(2,1)} %bitcast.9, bf16[1,4096,768]{2,1,0:T(8,128)(2,1)} %param.24), kind=kOutput, calls=%fused_computation.19 | convolution fusion | flops 3223584768 | bytes 12845056 | tf_op jit(solution)/shard_map/dot_general | solution.py:76
  133.5 8.4 %fusion = f32[16,2,16,4096]{3,2,1,0:T(8,128)} fusion(bf16[16,2,16,768]{3,2,1,0:T(8,128)(2,1)S(1)} %bitcast.78, bf16[1,768,4096]{2,1,0:T(8,128)(2,1)} %param.25), kind=kOutput, calls=%fused_computation | convolution fusion | flops 3221225472 | bytes 15466496 | tf_op jit(solution)/shard_map/dot_general | solution.py:139
  141.8 25.5 %all-reduce.2 = bf16[16,2,16,4096]{3,2,1,0:T(8,128)(2,1)} all-reduce(f32[16,2,16,4096]{3,2,1,0:T(8,128)} %fusion), channel_id=2, replica_groups=mesh['side'=2,'dev'=16] {'side'}, use_global_device_ids=true, to_apply=%region_12.13.clone | all-reduce | flops 2097152 | bytes 12582912
  167.3 3.8 %fusion.7 = bf16[16,16,4096]{2,1,0:T(8,128)(2,1)} fusion(bf16[16,2,16,4096]{3,2,1,0:T(8,128)(2,1)} %all-reduce.2, u32[]{:T(128)} %bitcast.24), kind=kLoop, calls=%fused_computation.12 | loop fusion | bytes 4194308 | tf_op jit(solution)/shard_map/convert_element_type | solution.py:145
  171.1 5.3 %all-to-all-start.1 = ((bf16[16,16,4096]{2,1,0:T(8,128)(2,1)}), bf16[16,16,4096]{2,1,0:T(8,128)(2,1)}, u32[]{:S(2)}, u32[]{:S(2)}) async-start(bf16[16,16,4096]{2,1,0:T(8,128)(2,1)} %fusion.7), calls=%async_computation.1 | async-start | bytes 4194304 | tf_op jit(solution)/shard_map/all_to_all | solution.py:144
  176.5 0.1 eq.88
  176.6 0.1 fusion.36
  176.7 0.2 reduce_window_sum.20
  176.9 0.2 select_reduce_fusion.3
  177.0 0.1 reduce_sum.80
  177.1 0.1 copy.55
  177.2 0.1 select_reduce_fusion
  177.4 47.7 %all-to-all-done.1 = bf16[16,16,4096]{2,1,0:T(8,128)(2,1)} async-done(((bf16[16,16,4096]{2,1,0:T(8,128)(2,1)}), bf16[16,16,4096]{2,1,0:T(8,128)(2,1)}, u32[]{:S(2)}, u32[]{:S(2)}) %all-to-all-start.1) | async-done | bytes 2097184 | tf_op jit(solution)/shard_map/all_to_all | solution.py:144
  225.1 3.2 %fusion.6 = bf16[16,4096]{1,0:T(8,128)(2,1)} fusion(f32[256,16]{0,1:T(8,128)S(1)} %select_reduce_fusion, bf16[256,4096]{1,0:T(8,128)(2,1)} %bitcast.17, bf16[16,4096]{1,0:T(8,128)(2,1)S(1)} %get-tuple-element.6), kind=kOutput, calls=%fused_computation.9 | convolution fusion | flops 201523200 | bytes 2375680 | tf_op jit(solution)/shard_map/dot_general | solution.py:148
  (25 shorter events, 0.4 us)
Async XLA Ops:
  0.0 2.7 %copy-start = (bf16[16,256,256]{2,1,0:T(8,128)(2,1)S(1)}, bf16[16,256,256]{2,1,0:T(8,128)(2,1)}, u32[]{:S(2)}) copy-start(bf16[16,256,256]{2,1,0:T(8,128)(2,1)} %param.14) | copy-start | bytes 6291460
  0.0 3.8 %copy-start.3 = (bf16[16,256]{1,0:T(8,128)(2,1)S(1)}, bf16[16,256]{1,0:T(8,128)(2,1)}, u32[]{:S(2)}) copy-start(bf16[16,256]{1,0:T(8,128)(2,1)} %param.17) | copy-start | bytes 24580
  3.9 2.1 copy-start.1
  3.9 2.4 %copy-start.4 = (bf16[4096]{0:T(1024)(128)(2,1)S(1)}, bf16[4096]{0:T(1024)(128)(2,1)}, u32[]{:S(2)}) copy-start(bf16[4096]{0:T(1024)(128)(2,1)} %param.20) | copy-start | bytes 24580
  3.9 4.5 %copy-start.2 = (s32[16,8]{0,1:T(8,128)S(1)}, s32[16,8]{0,1:T(8,128)}, u32[]{:S(2)}) copy-start(s32[16,8]{0,1:T(8,128)} %param.21) | copy-start | bytes 1540
  15.9 7.3 %copy-start.6 = (u32[32]{0:T(128)S(1)}, u32[32]{0:T(128)}, u32[]{:S(2)}) copy-start(u32[32]{0:T(128)} %constant.44) | copy-start | bytes 388
  15.9 102.9 %all-to-all-start = ((bf16[16,2,16,4096]{3,2,1,0:T(8,128)(2,1)}), bf16[16,2,16,4096]{3,2,1,0:T(8,128)(2,1)}, u32[]{:S(2)}, u32[]{:S(2)}) async-start(bf16[16,2,16,4096]{3,2,1,0:T(8,128)(2,1)} %pad_maximum_fusion), calls=%async_computation | async-start | bytes 8388608 | tf_op jit(solution)/shard_map/all_to_all | solution.py:137
  171.1 6.0 %copy-start.5 = (f32[16,8]{0,1:T(8,128)S(1)}, f32[16,8]{0,1:T(8,128)}, u32[]{:S(2)}) copy-start(f32[16,8]{0,1:T(8,128)} %param.22) | copy-start | bytes 1540
  171.1 54.0 %all-to-all-start.1 = ((bf16[16,16,4096]{2,1,0:T(8,128)(2,1)}), bf16[16,16,4096]{2,1,0:T(8,128)(2,1)}, u32[]{:S(2)}, u32[]{:S(2)}) async-start(bf16[16,16,4096]{2,1,0:T(8,128)(2,1)} %fusion.7), calls=%async_computation.1 | async-start | bytes 4194304 | tf_op jit(solution)/shard_map/all_to_all | solution.py:144
where the time goes:
time: 229 us; the launch traced here: 228 us
  waiting for transfers between devices  143 us (62%)
  matrix products  30.6 us (13%)
  blocking collectives  29.3 us (13%)
  starting transfers between devices  12.6 us (6%)
  local copies, waits for them, and re-layouts  7.35 us (3%)
  other arithmetic  5.45 us (2%)
    all_to_all x1, waiting for transfers between devices, on_device(): lax.all_to_all(outgoing, 'dev', split_axis=0, concat_axis=0, tiled=True)  95 us
    all_to_all x1, waiting for transfers between devices, on_device(): lax.all_to_all(summed.astype(jnp.bfloat16), 'dev', split_axis=0, concat_a...  47.7 us
    unnamed x1, blocking collectives  25.5 us
    dot_general x1, matrix products, on_device(): jnp.dot(act, down_proj[0], preferred_element_type=jnp.float32)  8.38 us
    dot_general x1, matrix products, expert_act(): up_val = jnp.dot(slot_rows, up_proj[0], preferred_element_type=jnp.float32)  7.55 us
    all_to_all x1, starting transfers between devices, on_device(): lax.all_to_all(outgoing, 'dev', split_axis=0, concat_axis=0, tiled=True)  7.27 us
    dot_general x1, matrix products, expert_act(): jnp.dot(slot_rows, gate_proj[0], preferred_element_type=jnp.float32)  7.04 us
    all_to_all x1, starting transfers between devices, on_device(): lax.all_to_all(summed.astype(jnp.bfloat16), 'dev', split_axis=0, concat_a...  5.31 us
  transfers between devices with their start and end apart: 2, of which 2 were waited for; matrix products, arithmetic and copies ran while one was open for 1% of the time, Pallas kernels for 0%

commit v1 on v0

--- a/solution.py
+++ b/solution.py
@@ -58,29 +58,15 @@
     return mixed.reshape(count_of_rows, QUERY_HEADS * HEAD_SIZE)
 
 
-def placement(chosen_ids, expert_count, slot_cap):
-    count_of_rows, top_count = chosen_ids.shape
-    flat_ids = chosen_ids.reshape(count_of_rows * top_count)
-    onehot = (flat_ids[:, None] == jnp.arange(expert_count, dtype=jnp.int32)[None, :]).astype(
-        jnp.int32
+def weight_columns(chosen_ids, gate_weights, expert_count):
+    experts = jnp.arange(expert_count, dtype=jnp.int32)
+    table = jnp.sum(
+        jnp.where(chosen_ids[:, :, None] == experts, gate_weights[:, :, None], 0.0), axis=1
     )
-    before = jnp.cumsum(onehot, axis=0) - onehot
-    slot_of = jnp.sum(before * onehot, axis=1)
-    target = flat_ids * slot_cap + slot_of
-    table = jnp.arange(expert_count * slot_cap, dtype=jnp.int32)[:, None] == target[None, :]
-    return table.reshape(expert_count * slot_cap, count_of_rows, top_count)
-
-
-def expert_act(slot_rows, gate_proj, up_proj):
-    gate_val = jnp.dot(slot_rows, gate_proj[0], preferred_element_type=jnp.float32)
-    up_val = jnp.dot(slot_rows, up_proj[0], preferred_element_type=jnp.float32)
-    return (jax.nn.silu(gate_val) * up_val).astype(jnp.bfloat16)
-
-
-def pack_rows(table, normed, expert_count, slot_cap):
-    spread = jnp.sum(table, axis=2).astype(jnp.bfloat16)
-    filled = jnp.dot(spread, normed, preferred_element_type=jnp.float32).astype(jnp.bfloat16)
-    return filled.reshape(expert_count, slot_cap, normed.shape[1])
+    high = table.astype(jnp.bfloat16)
+    low = (table - high.astype(jnp.float32)).astype(jnp.bfloat16)
+    columns = jnp.concatenate([high, low], axis=1)
+    return jnp.pad(columns, ((0, 0), (0, -columns.shape[1] % 128)))
 
 
 def on_device(
@@ -99,9 +85,7 @@
     down_proj,
 ):
     count_of_rows, width = residual.shape
-    top_count = expert_ids.shape[1]
     expert_count = lax.axis_size("dev")
-    slot_cap = min(count_of_rows, max(6, 2 * count_of_rows * top_count // expert_count))
     attn = attend(
         queries,
         cached_key_table,
@@ -116,39 +100,24 @@
     normed = (wide * lax.rsqrt(mean_square + 1e-06) * norm_gain.astype(jnp.float32)).astype(
         jnp.bfloat16
     )
-    own_table = placement(expert_ids, expert_count, slot_cap)
-    both_normed, both_ids = (
-        lax.all_gather(normed, "side", axis=0, tiled=True),
-        lax.all_gather(expert_ids, "side", axis=0, tiled=True),
+    mine = lax.axis_index("dev")
+    sent = jnp.concatenate([normed, weight_columns(expert_ids, gate_weights, expert_count)], axis=1)
+    rows = lax.all_gather(sent, ("side", "dev"), axis=0, tiled=True)
+    tail = rows[:, width:].astype(jnp.float32)
+    places = jnp.arange(tail.shape[1], dtype=jnp.int32)
+    weight = jnp.sum(
+        jnp.where((places == mine) | (places == mine + expert_count), tail, 0.0),
+        axis=1,
+        keepdims=True,
     )
-    first_block = pack_rows(
-        placement(both_ids[:count_of_rows], expert_count, slot_cap),
-        both_normed[:count_of_rows],
-        expert_count,
-        slot_cap,
-    )
-    second_block = pack_rows(
-        placement(both_ids[count_of_rows:], expert_count, slot_cap),
-        both_normed[count_of_rows:],
-        expert_count,
-        slot_cap,
-    )
-    outgoing = jnp.stack([first_block, second_block], axis=1)
-    arrived = lax.all_to_all(outgoing, "dev", split_axis=0, concat_axis=0, tiled=True)
-    act = expert_act(arrived.reshape(-1, width), gate_proj, up_proj)
-    partial_value = jnp.dot(act, down_proj[0], preferred_element_type=jnp.float32)
-    partial_value = partial_value.reshape(expert_count, 2, slot_cap, width)
-    summed = lax.psum_scatter(partial_value, "side", scatter_dimension=1, tiled=True).reshape(
-        expert_count, slot_cap, width
-    )
-    returned = lax.all_to_all(
-        summed.astype(jnp.bfloat16), "dev", split_axis=0, concat_axis=0, tiled=True
-    )
-    combine = jnp.sum(own_table.astype(jnp.float32) * gate_weights[None, :, :], axis=2)
-    moe_sum = jnp.dot(
-        combine.T, returned.reshape(-1, width).astype(jnp.float32), precision=lax.Precision.HIGHEST
-    )
-    return (hidden.astype(jnp.float32) + moe_sum).astype(jnp.bfloat16)
+    rows = rows[:, :width]
+    gate_val = jnp.dot(rows, gate_proj[0], preferred_element_type=jnp.float32)
+    up_val = jnp.dot(rows, up_proj[0], preferred_element_type=jnp.float32)
+    act = (jax.nn.silu(gate_val) * up_val).astype(jnp.bfloat16)
+    part = jnp.dot(act, down_proj[0], preferred_element_type=jnp.float32)
+    part = (part * weight).astype(jnp.bfloat16)
+    summed = lax.psum_scatter(part, ("side", "dev"), scatter_dimension=0, tiled=True)
+    return (hidden.astype(jnp.float32) + summed.astype(jnp.float32)).astype(jnp.bfloat16)
 
 
 def solution(mesh):

time: 229 us -> 261 us (1.14)
  the two profiles are of different devices: /device:TPU:14 before, /device:TPU:0 now
where the time goes in v1:
time: 261 us
  waiting for transfers between devices  209 us (80%)
  matrix products  28.7 us (11%)
  between operations  13.5 us (5%)
  other arithmetic  5.76 us (2%)
  local copies, waits for them, and re-layouts  3.87 us (1%)
    reduce_scatter x1, waiting for transfers between devices, on_device(): lax.psum_scatter(part, ('side', 'dev'), scatter_dimension=0, tiled=True)  144 us
    all_gather x1, waiting for transfers between devices, on_device(): rows = lax.all_gather(sent, ('side', 'dev'), axis=0, tiled=True)  65.3 us
    dot_general x1, matrix products, on_device(): part = jnp.dot(act, down_proj[0], preferred_element_type=jnp.float32)  17.1 us
    dot_general x1, matrix products, on_device(): gate_val = jnp.dot(rows, gate_proj[0], preferred_element_type=jnp.float32)  8.68 us
  transfers between devices with their start and end apart: 2, of which 2 were waited for; matrix products, arithmetic and copies ran while one was open for 0% of the time, Pallas kernels for 0%

profile of v1, /device:TPU:0, one launch (start us, length us, event | category | flops | bytes accessed | tf_op | source)
XLA Modules:
  0.0 260.8 jit_solution(9366525712988929243)
XLA Ops:
  6.5 0.0 copy-start
  6.5 0.0 all-gather.2.cloned.1.call-start
  6.5 0.9 iota_compare_fusion.1
  7.4 0.8 copy.20
  8.2 0.8 copy.21
  8.9 0.1 select_reduce_fusion.1
  9.1 0.7 reshape.64
  9.8 0.7 reshape.60
  10.5 0.7 convert_element_type.69
  11.2 0.9 copy.26
  12.1 0.2 fusion.47
  12.3 0.0 copy-done
  12.3 0.0 copy-start.1
  12.3 0.8 fusion.46
  13.1 0.3 fusion.31
  13.4 2.1 fusion.27
  15.5 0.0 copy-done.1
  15.5 0.3 fusion.32
  15.8 0.1 fusion.42
  15.8 0.1 fusion.34
  16.0 0.7 pad_maximum_fusion
  16.6 0.0 all-gather.2.cloned.1.call-update
  16.6 0.0 reduce-scatter.2.cloned.1.call-start
  16.7 65.3 %all-gather.2.cloned.1.call-done = bf16[512,4224]{1,0:T(8,128)(2,1)} async-done(((bf16[16,4224]{1,0:T(8,128)(2,1)}), bf16[512,4224]{1,0:T(8,128)(2,1)}) %all-gather.2.cloned.1.call-update) | async-done | bytes 4325392 | tf_op jit(solution)/shard_map/all_gather | solution.py:105
  82.0 1.0 select_reduce_fusion
  83.0 8.7 %fusion.3 = f32[512,768]{1,0:T(8,128)} fusion(bf16[1,4096,768]{2,1,0:T(8,128)(2,1)} %param.23, bf16[512,4224]{1,0:T(8,128)(2,1)} %all-gather.2.cloned.1.call-done), kind=kOutput, calls=%fused_computation.4 | convolution fusion | flops 3221225472 | bytes 12058624 | tf_op jit(solution)/shard_map/dot_general | solution.py:114
  91.7 17.1 %multiply_convert_fusion = bf16[512,4096]{1,0:T(8,128)(2,1)} fusion(bf16[1,768,4096]{2,1,0:T(8,128)(2,1)} %param.25, f32[512]{0:T(512)S(1)} %select_reduce_fusion, f32[512,768]{1,0:T(8,128)} %fusion.3, bf16[1,4096,768]{2,1,0:T(8,128)(2,1)} %param.24, bf16[512,4224]{1,0:T(8,128)(2,1)} %all-gather.2.cloned.1.call-done), kind=kOutput, calls=%fused_computation | convolution fusion | flops 6449004544 | bytes 22546432 | tf_op jit(solution)/shard_map/dot_general | solution.py:117
  108.8 0.0 reduce-scatter.2.cloned.1.call-update
  108.8 143.6 %reduce-scatter.2.cloned.1.call-done = bf16[16,4096]{1,0:T(8,128)(2,1)} async-done(((bf16[512,4096]{1,0:T(8,128)(2,1)}), bf16[16,4096]{1,0:T(8,128)(2,1)}) %reduce-scatter.2.cloned.1.call-update) | async-done | bytes 131088 | tf_op jit(solution)/shard_map/reduce_scatter | solution.py:119
  252.4 1.6 fusion.35
  (5 shorter events, 0.1 us)
Async XLA Ops:
  6.5 5.7 %copy-start = (bf16[16,256,256]{2,1,0:T(8,128)(2,1)S(1)}, bf16[16,256,256]{2,1,0:T(8,128)(2,1)}, u32[]{:S(2)}) copy-start(bf16[16,256,256]{2,1,0:T(8,128)(2,1)} %param.14) | copy-start | bytes 6291460
  6.5 75.5 %all-gather.2.cloned.1.call-start = ((), (), s32[]{:S(2)}) async-start(), calls=%async_computation.1 | async-start | bytes 4460544 | tf_op jit(solution)/shard_map/all_gather | solution.py:105
  12.3 3.2 %copy-start.1 = (bf16[16,4096]{1,0:T(8,128)(2,1)S(1)}, bf16[16,4096]{1,0:T(8,128)(2,1)}, u32[]{:S(2)}) copy-start(bf16[16,4096]{1,0:T(8,128)(2,1)} %param.19) | copy-start | bytes 393220
  16.6 235.8 %reduce-scatter.2.cloned.1.call-start = ((), (), s32[]{:S(2)}) async-start(), calls=%async_computation.2 | async-start | bytes 4325376 | tf_op jit(solution)/shard_map/reduce_scatter | solution.py:119
Sparse Core Ops, SparseCore 0:
  16.8 65.2 all-gather.1
  108.9 143.4 reduce-scatter.1

commit v2 on v1

--- a/solution.py
+++ b/solution.py
@@ -1,11 +1,302 @@
+import functools
+
 import jax
 import jax.numpy as jnp
 from jax import lax
+from jax.experimental import pallas as pl
+from jax.experimental.pallas import tpu as pltpu
 from jax.sharding import PartitionSpec as P
 
 QUERY_HEADS = 32
 KEY_VALUE_HEADS = 2
 HEAD_SIZE = 128
+MESH = pl.DeviceIdType.MESH
+VMEM_LIMIT = 60 * 1024 * 1024
+
+
+def grid_of(count):
+    return {16: (4, 2, 2), 64: (4, 4, 4)}.get(count, (count, 1, 1))
+
+
+def halves_of(width):
+    first = width // 256 * 128
+    return (slice(0, first), slice(first, width))
+
+
+class Links:
+    def __init__(self, sizes):
+        self.sizes = sizes
+        me = lax.axis_index("dev")
+        self.side = lax.axis_index("side")
+        self.at = (me // (sizes[1] * sizes[2]), me // sizes[2] % sizes[1], me % sizes[2])
+        self.started = []
+
+    def moved(self, steps):
+        spot = [(a + n + d) % n for a, d, n in zip(self.at, steps, self.sizes)]
+        return (spot[0] * self.sizes[1] + spot[1]) * self.sizes[2] + spot[2]
+
+    def along(self, axis, step):
+        return {"dev": self.moved(tuple(step if i == axis else 0 for i in range(3)))}
+
+    def other(self):
+        return {"side": 1 - self.side}
+
+    def barrier(self):
+        semaphore = pltpu.get_barrier_semaphore()
+        peers = [self.other()]
+        for axis in range(3):
+            peers += [self.along(axis, step) for step in range(1, self.sizes[axis])]
+        for peer in peers:
+            pl.semaphore_signal(semaphore, inc=1, device_id=peer, device_id_type=MESH)
+        pl.semaphore_wait(semaphore, len(peers))
+
+    def copy(self, source, target, send_sems, recv_sem, peer):
+        sent = pltpu.make_async_remote_copy(
+            src_ref=source,
+            dst_ref=target,
+            send_sem=send_sems.at[len(self.started)],
+            recv_sem=recv_sem,
+            device_id=peer,
+            device_id_type=MESH,
+        )
+        sent.start()
+        self.started.append(sent)
+
+    def arrived(self, target, send_sems, recv_sem):
+        pltpu.make_async_remote_copy(
+            src_ref=target,
+            dst_ref=target,
+            send_sem=send_sems.at[0],
+            recv_sem=recv_sem,
+            device_id=self.other(),
+            device_id_type=MESH,
+        ).wait_recv()
+
+    def finish(self):
+        for sent in self.started:
+            sent.wait_send()
+
+
+def gather_kernel(sizes, own_ref, all_ref, send_sems, near_sems, mid_sems, far_sems, side_sems):
+    n0, n1, n2 = sizes
+    count = n0 * n1 * n2
+    links = Links(sizes)
+    cuts = halves_of(own_ref.shape[1])
+    links.barrier()
+
+    def block(steps, half, side=None):
+        base = (links.side if side is None else side) * count
+        return all_ref.at[base + links.moved(steps), :, cuts[half]]
+
+    def source(steps, half):
+        return own_ref.at[:, cuts[half]] if steps == (0, 0, 0) else block(steps, half)
+
+    def relative(steps):
+        back = [-d % n for d, n in zip(steps, sizes)]
+        return (back[0] * n1 + back[1]) * n2 + back[2]
+
+    def cross(steps, half):
+        links.copy(
+            source(steps, half), block(steps, half), send_sems,
+            side_sems.at[half, relative(steps)], links.other(),
+        )
+
+    def spread(steps, half, axis, sems, slot):
+        for k in range(1, sizes[axis]):
+            links.copy(
+                source(steps, half), block(steps, half), send_sems,
+                sems.at[half, slot * max(sizes) + k], links.along(axis, k),
+            )
+
+    first, second = (2, 1), (1, 2)
+    for half in range(2):
+        for k in range(1, n0):
+            links.copy(
+                source((0, 0, 0), half), block((0, 0, 0), half), send_sems,
+                near_sems.at[half, k], links.along(0, k),
+            )
+    for j in range(n0):
+        for half in range(2):
+            steps = (-j, 0, 0)
+            if j:
+                links.arrived(block(steps, half), send_sems, near_sems.at[half, j])
+            spread(steps, half, first[half], mid_sems, j)
+            spread(steps, half, second[half], far_sems, j * max(sizes))
+            cross(steps, half)
+
+    def shifted(j, half, mid, far):
+        steps = [-j, 0, 0]
+        steps[first[half]] = -mid
+        steps[second[half]] = -far
+        return tuple(steps)
+
+    for j in range(n0):
+        for half in range(2):
+            for k in range(1, sizes[first[half]]):
+                steps = shifted(j, half, k, 0)
+                links.arrived(block(steps, half), send_sems, mid_sems.at[half, j * max(sizes) + k])
+                spread(steps, half, second[half], far_sems, j * max(sizes) + k)
+                cross(steps, half)
+    for j in range(n0):
+        for c in range(max(sizes)):
+            for half in range(2):
+                if c >= sizes[first[half]]:
+                    continue
+                for k in range(1, sizes[second[half]]):
+                    steps = shifted(j, half, c, k)
+                    slot = (j * max(sizes) + c) * max(sizes) + k
+                    links.arrived(block(steps, half), send_sems, far_sems.at[half, slot])
+                    cross(steps, half)
+    all_ref[links.side * count + links.moved((0, 0, 0))] = own_ref[...]
+    for j in range(n0):
+        for b in range(n1):
+            for c in range(n2):
+                for half in range(2):
+                    steps = (-j, -b, -c)
+                    links.arrived(
+                        block(steps, half, 1 - links.side), send_sems,
+                        side_sems.at[half, relative(steps)],
+                    )
+    links.finish()
+
+
+def gather_rows(own):
+    count = lax.axis_size("dev")
+    sizes = grid_of(count)
+    wide = max(sizes)
+    rows, width = own.shape
+    dma = pltpu.SemaphoreType.DMA
+    sends = 2 * (count - 1) + 2 * count
+    return pl.pallas_call(
+        functools.partial(gather_kernel, sizes),
+        out_shape=jax.ShapeDtypeStruct((2 * count, rows, width), own.dtype),
+        in_specs=[pl.BlockSpec(memory_space=pltpu.VMEM)],
+        out_specs=pl.BlockSpec(memory_space=pltpu.VMEM),
+        scratch_shapes=[
+            dma((sends,)),
+            dma((2, wide)),
+            dma((2, wide * wide)),
+            dma((2, wide * wide * wide)),
+            dma((2, count)),
+        ],
+        compiler_params=pltpu.CompilerParams(
+            collective_id=0, has_side_effects=True, vmem_limit_bytes=VMEM_LIMIT
+        ),
+        name="gather_rows",
+    )(own).reshape(2 * count * rows, width)
+
+
+def sum_kernel(
+    sizes, part_ref, out_ref, acc, from_side, from_far, from_mid, from_near,
+    send_sems, side_sems, far_sems, mid_sems, near_sems,
+):
+    n0, n1, n2 = sizes
+    count = n0 * n1 * n2
+    wide = max(sizes)
+    links = Links(sizes)
+    cuts = halves_of(out_ref.shape[1])
+    first, second = (2, 1), (1, 2)
+    links.barrier()
+    order = [(j, b, c) for b in range(n1 - 1, -1, -1) for c in range(n2 - 1, -1, -1) for j in range(n0)]
+
+    def mine(steps):
+        return links.moved(steps)
+
+    for i, steps in enumerate(order):
+        links.copy(
+            part_ref.at[(1 - links.side) * count + mine(steps)], from_side.at[i],
+            send_sems, side_sems.at[i], links.other(),
+        )
+
+    def total(left, right):
+        return (left.astype(jnp.float32) + right.astype(jnp.float32)).astype(jnp.bfloat16)
+
+    for i, steps in enumerate(order):
+        spot = mine(steps)
+        links.arrived(from_side.at[i], send_sems, side_sems.at[i])
+        acc[spot] = total(part_ref[links.side * count + spot], from_side[i])
+        for half in range(2):
+            k = steps[second[half]]
+            if k:
+                slot = (steps[0] * wide + steps[first[half]]) * wide + k
+                links.copy(
+                    acc.at[spot, :, cuts[half]], from_far.at[half, slot],
+                    send_sems, far_sems.at[half, slot], links.along(second[half], k),
+                )
+
+    def shifted(j, half, mid):
+        steps = [j, 0, 0]
+        steps[first[half]] = mid
+        return tuple(steps)
+
+    for c in range(wide - 1, -1, -1):
+        for j in range(n0):
+            for half in range(2):
+                if c >= sizes[first[half]]:
+                    continue
+                spot = mine(shifted(j, half, c))
+                for k in range(1, sizes[second[half]]):
+                    slot = (j * wide + c) * wide + k
+                    links.arrived(from_far.at[half, slot], send_sems, far_sems.at[half, slot])
+                    acc[spot, :, cuts[half]] = total(
+                        acc[spot, :, cuts[half]], from_far[half, slot]
+                    )
+                if c:
+                    slot = j * wide + c
+                    links.copy(
+                        acc.at[spot, :, cuts[half]], from_mid.at[half, slot],
+                        send_sems, mid_sems.at[half, slot], links.along(first[half], c),
+                    )
+    for j in range(n0 - 1, -1, -1):
+        for half in range(2):
+            spot = mine((j, 0, 0))
+            for k in range(1, sizes[first[half]]):
+                slot = j * wide + k
+                links.arrived(from_mid.at[half, slot], send_sems, mid_sems.at[half, slot])
+                acc[spot, :, cuts[half]] = total(acc[spot, :, cuts[half]], from_mid[half, slot])
+            if j:
+                links.copy(
+                    acc.at[spot, :, cuts[half]], from_near.at[half, j],
+                    send_sems, near_sems.at[half, j], links.along(0, j),
+                )
+    for half in range(2):
+        value = acc[mine((0, 0, 0)), :, cuts[half]].astype(jnp.float32)
+        for k in range(1, n0):
+            links.arrived(from_near.at[half, k], send_sems, near_sems.at[half, k])
+            value = value + from_near[half, k].astype(jnp.float32)
+        out_ref[:, cuts[half]] = value
+    links.finish()
+
+
+def sum_rows(part):
+    count = lax.axis_size("dev")
+    sizes = grid_of(count)
+    wide = max(sizes)
+    _, rows, width = part.shape
+    dma = pltpu.SemaphoreType.DMA
+    slots = sizes[0] * wide
+    return pl.pallas_call(
+        functools.partial(sum_kernel, sizes),
+        out_shape=jax.ShapeDtypeStruct((rows, width), jnp.float32),
+        in_specs=[pl.BlockSpec(memory_space=pltpu.VMEM)],
+        out_specs=pl.BlockSpec(memory_space=pltpu.VMEM),
+        scratch_shapes=[
+            pltpu.VMEM((count, rows, width), part.dtype),
+            pltpu.VMEM((count, rows, width), part.dtype),
+            pltpu.VMEM((2, slots * wide, rows, width // 2), part.dtype),
+            pltpu.VMEM((2, slots, rows, width // 2), part.dtype),
+            pltpu.VMEM((2, sizes[0], rows, width // 2), part.dtype),
+            dma((count + 2 * (count - 1),)),
+            dma((count,)),
+            dma((2, slots * wide)),
+            dma((2, slots)),
+            dma((2, sizes[0])),
+        ],
+        compiler_params=pltpu.CompilerParams(
+            collective_id=1, has_side_effects=True, vmem_limit_bytes=VMEM_LIMIT
+        ),
+        name="sum_rows",
+    )(part)
 
 
 def attend(
@@ -102,7 +393,7 @@
     )
     mine = lax.axis_index("dev")
     sent = jnp.concatenate([normed, weight_columns(expert_ids, gate_weights, expert_count)], axis=1)
-    rows = lax.all_gather(sent, ("side", "dev"), axis=0, tiled=True)
+    rows = gather_rows(sent)
     tail = rows[:, width:].astype(jnp.float32)
     places = jnp.arange(tail.shape[1], dtype=jnp.int32)
     weight = jnp.sum(
@@ -116,8 +407,8 @@
     act = (jax.nn.silu(gate_val) * up_val).astype(jnp.bfloat16)
     part = jnp.dot(act, down_proj[0], preferred_element_type=jnp.float32)
     part = (part * weight).astype(jnp.bfloat16)
-    summed = lax.psum_scatter(part, ("side", "dev"), scatter_dimension=0, tiled=True)
-    return (hidden.astype(jnp.float32) + summed.astype(jnp.float32)).astype(jnp.bfloat16)
+    summed = sum_rows(part.reshape(-1, count_of_rows, width))
+    return (hidden.astype(jnp.float32) + summed).astype(jnp.bfloat16)
 
 
 def solution(mesh):

time: 261 us -> 115 us (0.44)
  waiting for transfers between devices: 209 us -> 0 us
  Pallas kernels: 0 us -> 76.1 us
  between operations: 13.5 us -> 0.09 us
    reduce_scatter x1 -> x0, waiting for transfers between devices: 144 us -> none  [on_device(): lax.psum_scatter(part, ('side', 'dev'), scatter_dimension=0, tiled=True)]
    pallas_call x0 -> x2, Pallas kernels: none -> 76.1 us  [the longest x1 41.2 us: sum_rows(): pl.pallas_call(functools.partial(sum_kernel, sizes), out_shape=jax.ShapeD...]
    all_gather x1 -> x0, waiting for transfers between devices: 65.3 us -> none  [on_device(): rows = lax.all_gather(sent, ('side', 'dev'), axis=0, tiled=True)]
  transfers between devices with their start and end apart: 2 -> 0, of which waited for: 2 -> 0; matrix products, arithmetic and copies ran while one was open for 0% -> 0% of each run, Pallas kernels for 0% -> 0%
where the time goes in v2:
time: 115 us
  Pallas kernels  76.1 us (66%)
  matrix products  28.7 us (25%)
  other arithmetic  5.81 us (5%)
  local copies, waits for them, and re-layouts  3.86 us (3%)
    pallas_call x1, Pallas kernels, sum_rows(): pl.pallas_call(functools.partial(sum_kernel, sizes), out_shape=jax.ShapeD...  41.2 us
    pallas_call x1, Pallas kernels, gather_rows(): pl.pallas_call(functools.partial(gather_kernel, sizes), out_shape=jax.Sha...  34.8 us
    dot_general x1, matrix products, on_device(): part = jnp.dot(act, down_proj[0], preferred_element_type=jnp.float32)  17 us
    dot_general x1, matrix products, on_device(): gate_val = jnp.dot(rows, gate_proj[0], preferred_element_type=jnp.float32)  8.69 us
    unnamed x7, local copies, waits for them, and re-layouts  2.45 us

profile of v2, /device:TPU:0, one launch (start us, length us, event | category | flops | bytes accessed | tf_op | source)
XLA Modules:
  0.0 114.5 jit_solution(11893076375349018174)
XLA Ops:
  0.0 0.0 copy-start
  0.0 0.9 iota_compare_fusion.1
  0.9 0.8 copy.20
  1.6 0.8 copy.21
  2.4 0.1 select_reduce_fusion.1
  2.5 0.1 fusion.42
  2.6 0.7 reshape.72
  3.3 0.7 reshape.68
  4.0 0.7 convert_element_type.66
  4.7 0.9 copy.26
  5.7 0.2 fusion.47
  5.8 0.0 copy-done
  5.8 0.0 copy-start.1
  5.8 0.8 fusion.46
  6.6 0.3 fusion.31
  7.0 2.0 %fusion.27 = f32[16,2,16,128]{3,2,1,0:T(8,128)S(1)} fusion(f32[16,2,16,256]{3,2,1,0:T(8,128)S(1)} %get-tuple-element.12, f32[16,2,16]{2,1,0:T(2,128)S(1)} %get-tuple-element.10, f32[16,2,16]{2,1,0:T(2,128)S(1)} %multiply_maximum_fusion, f32[16,2,128]{2,1,0:T(2,128)S(1)} %reshape.68, f32[16,2,16]{2,1,0:T(2,128)S(1)} %get-tuple-element.9, ...), kind=kOutput, calls=%fused_computation.17 | convolution fusion | flops 34078720 | bytes 2906112 | tf_op jit(solution)/shard_map/rkgl,rlkd->rkgd/dot_general | solution.py:341
  9.0 0.0 copy-done.1
  9.0 0.3 fusion.32
  9.3 0.1 fusion.34
  9.4 0.7 pad_maximum_fusion.own_ref
  10.1 34.8 %gather_rows.1 = bf16[32,16,4224]{2,1,0:T(8,128)(2,1)} custom-call(bf16[16,4224]{1,0:T(8,128)(2,1)} %pad_maximum_fusion.own_ref), custom_call_target="tpu_custom_call" | custom-call | tf_op jit(solution)/shard_map/gather_rows/pallas_call | solution.py:170
  44.9 1.0 select_reduce_fusion
  45.9 8.7 %fusion.3 = f32[512,768]{1,0:T(8,128)} fusion(bf16[1,4096,768]{2,1,0:T(8,128)(2,1)} %param.23, bf16[512,4224]{1,0:T(8,128)(2,1)} %bitcast.53), kind=kOutput, calls=%fused_computation.4 | convolution fusion | flops 3221225472 | bytes 12058624 | tf_op jit(solution)/shard_map/dot_general | solution.py:405
  54.6 17.0 %multiply_convert_fusion = bf16[512,4096]{1,0:T(8,128)(2,1)} fusion(bf16[1,768,4096]{2,1,0:T(8,128)(2,1)} %param.25, f32[512]{0:T(512)S(1)} %select_reduce_fusion, f32[512,768]{1,0:T(8,128)} %fusion.3, bf16[1,4096,768]{2,1,0:T(8,128)(2,1)} %param.24, bf16[512,4224]{1,0:T(8,128)(2,1)} %bitcast.54), kind=kOutput, calls=%fused_computation | convolution fusion | flops 6449004544 | bytes 22546432 | tf_op jit(solution)/shard_map/dot_general | solution.py:408
  71.6 41.2 %sum_rows.1 = f32[16,4096]{1,0:T(8,128)} custom-call(bf16[32,16,4096]{2,1,0:T(8,128)(2,1)} %bitcast.55), custom_call_target="tpu_custom_call" | custom-call | tf_op jit(solution)/shard_map/sum_rows/pallas_call | solution.py:278
  112.9 1.6 %fusion.35 = bf16[16,4096]{1,0:T(8,128)(2,1)} fusion(f32[16,4096]{1,0:T(8,128)} %sum_rows.1, bf16[16,4096]{1,0:T(8,128)(2,1)S(1)} %get-tuple-element.6), kind=kLoop, calls=%fused_computation.28 | loop fusion | flops 196608 | bytes 524288 | tf_op jit(solution)/shard_map/convert_element_type | solution.py:411
  (5 shorter events, 0.1 us)
Async XLA Ops:
  0.0 5.8 %copy-start = (bf16[16,256,256]{2,1,0:T(8,128)(2,1)S(1)}, bf16[16,256,256]{2,1,0:T(8,128)(2,1)}, u32[]{:S(2)}) copy-start(bf16[16,256,256]{2,1,0:T(8,128)(2,1)} %param.14) | copy-start | bytes 6291460
  5.8 3.2 %copy-start.1 = (bf16[16,4096]{1,0:T(8,128)(2,1)S(1)}, bf16[16,4096]{1,0:T(8,128)(2,1)}, u32[]{:S(2)}) copy-start(bf16[16,4096]{1,0:T(8,128)(2,1)} %param.19) | copy-start | bytes 393220

commit v3 on v2

--- a/solution.py
+++ b/solution.py
@@ -299,6 +299,332 @@
     )(part)
 
 
+def gather_steps(sizes, links, halfway, own_ref, all_ref, send_sems, near_sems, mid_sems, far_sems, side_sems):
+    n0, n1, n2 = sizes
+    count = n0 * n1 * n2
+    cuts = halves_of(own_ref.shape[1])
+
+    def block(steps, half, side=None):
+        base = (links.side if side is None else side) * count
+        return all_ref.at[base + links.moved(steps), :, cuts[half]]
+
+    def source(steps, half):
+        return own_ref.at[:, cuts[half]] if steps == (0, 0, 0) else block(steps, half)
+
+    def relative(steps):
+        back = [-d % n for d, n in zip(steps, sizes)]
+        return (back[0] * n1 + back[1]) * n2 + back[2]
+
+    def cross(steps, half):
+        links.copy(
+            source(steps, half), block(steps, half), send_sems,
+            side_sems.at[half, relative(steps)], links.other(),
+        )
+
+    def spread(steps, half, axis, sems, slot):
+        for k in range(1, sizes[axis]):
+            links.copy(
+                source(steps, half), block(steps, half), send_sems,
+                sems.at[half, slot * max(sizes) + k], links.along(axis, k),
+            )
+
+    first, second = (2, 1), (1, 2)
+    for half in range(2):
+        for k in range(1, n0):
+            links.copy(
+                source((0, 0, 0), half), block((0, 0, 0), half), send_sems,
+                near_sems.at[half, k], links.along(0, k),
+            )
+    for j in range(n0):
+        for half in range(2):
+            steps = (-j, 0, 0)
+            if j:
+                links.arrived(block(steps, half), send_sems, near_sems.at[half, j])
+            spread(steps, half, first[half], mid_sems, j)
+            spread(steps, half, second[half], far_sems, j * max(sizes))
+            cross(steps, half)
+
+    def shifted(j, half, mid, far):
+        steps = [-j, 0, 0]
+        steps[first[half]] = -mid
+        steps[second[half]] = -far
+        return tuple(steps)
+
+    for j in range(n0):
+        for half in range(2):
+            for k in range(1, sizes[first[half]]):
+                steps = shifted(j, half, k, 0)
+                links.arrived(block(steps, half), send_sems, mid_sems.at[half, j * max(sizes) + k])
+                spread(steps, half, second[half], far_sems, j * max(sizes) + k)
+                cross(steps, half)
+    all_ref[links.side * count + links.moved((0, 0, 0))] = own_ref[...]
+    pending = {(b, c, half) for b in range(n1) for c in range(n2) for half in range(2)}
+
+    def crossed(b, c, half):
+        if (b, c, half) in pending:
+            pending.remove((b, c, half))
+            for j in range(n0):
+                steps = (-j, -b, -c)
+                links.arrived(
+                    block(steps, half, 1 - links.side), send_sems,
+                    side_sems.at[half, relative(steps)],
+                )
+
+    for c in range(n2):
+        crossed(0, c, 0)
+    halfway(0)
+    for j in range(n0):
+        if j == n0 // 2:
+            for b in range(n1):
+                crossed(b, 0, 1)
+            halfway(1)
+        for c in range(max(sizes)):
+            for half in range(2):
+                if c >= sizes[first[half]]:
+                    continue
+                for k in range(1, sizes[second[half]]):
+                    steps = shifted(j, half, c, k)
+                    slot = (j * max(sizes) + c) * max(sizes) + k
+                    links.arrived(block(steps, half), send_sems, far_sems.at[half, slot])
+                    cross(steps, half)
+    for b in range(n1):
+        for c in range(n2):
+            for half in range(2):
+                crossed(b, c, half)
+
+
+def sum_steps(
+    sizes, links, ready, part_ref, out_ref, acc, from_side, from_far, from_mid, from_near,
+    send_sems, side_sems, far_sems, mid_sems, near_sems,
+):
+    n0, n1, n2 = sizes
+    count = n0 * n1 * n2
+    wide = max(sizes)
+    cuts = halves_of(out_ref.shape[1])
+    first, second = (2, 1), (1, 2)
+    order = [(j, b, c) for b in range(n1 - 1, -1, -1) for c in range(n2 - 1, -1, -1) for j in range(n0)]
+
+    def mine(steps):
+        return links.moved(steps)
+
+    sent_to = None
+    for i, steps in enumerate(order):
+        if steps[1] != sent_to:
+            sent_to = steps[1]
+            ready(sent_to)
+        links.copy(
+            part_ref.at[(1 - links.side) * count + mine(steps)], from_side.at[i],
+            send_sems, side_sems.at[i], links.other(),
+        )
+
+    def total(left, right):
+        return (left.astype(jnp.float32) + right.astype(jnp.float32)).astype(jnp.bfloat16)
+
+    for i, steps in enumerate(order):
+        spot = mine(steps)
+        links.arrived(from_side.at[i], send_sems, side_sems.at[i])
+        acc[spot] = total(part_ref[links.side * count + spot], from_side[i])
+        for half in range(2):
+            k = steps[second[half]]
+            if k:
+                slot = (steps[0] * wide + steps[first[half]]) * wide + k
+                links.copy(
+                    acc.at[spot, :, cuts[half]], from_far.at[half, slot],
+                    send_sems, far_sems.at[half, slot], links.along(second[half], k),
+                )
+
+    def shifted(j, half, mid):
+        steps = [j, 0, 0]
+        steps[first[half]] = mid
+        return tuple(steps)
+
+    for c in range(wide - 1, -1, -1):
+        for j in range(n0):
+            for half in range(2):
+                if c >= sizes[first[half]]:
+                    continue
+                spot = mine(shifted(j, half, c))
+                for k in range(1, sizes[second[half]]):
+                    slot = (j * wide + c) * wide + k
+                    links.arrived(from_far.at[half, slot], send_sems, far_sems.at[half, slot])
+                    acc[spot, :, cuts[half]] = total(
+                        acc[spot, :, cuts[half]], from_far[half, slot]
+                    )
+                if c:
+                    slot = j * wide + c
+                    links.copy(
+                        acc.at[spot, :, cuts[half]], from_mid.at[half, slot],
+                        send_sems, mid_sems.at[half, slot], links.along(first[half], c),
+                    )
+    for j in range(n0 - 1, -1, -1):
+        for half in range(2):
+            spot = mine((j, 0, 0))
+            for k in range(1, sizes[first[half]]):
+                slot = j * wide + k
+                links.arrived(from_mid.at[half, slot], send_sems, mid_sems.at[half, slot])
+                acc[spot, :, cuts[half]] = total(acc[spot, :, cuts[half]], from_mid[half, slot])
+            if j:
+                links.copy(
+                    acc.at[spot, :, cuts[half]], from_near.at[half, j],
+                    send_sems, near_sems.at[half, j], links.along(0, j),
+                )
+    for half in range(2):
+        value = acc[mine((0, 0, 0)), :, cuts[half]].astype(jnp.float32)
+        for k in range(1, n0):
+            links.arrived(from_near.at[half, k], send_sems, near_sems.at[half, k])
+            value = value + from_near[half, k].astype(jnp.float32)
+        out_ref[:, cuts[half]] = value
+
+
+def layer_kernel(
+    sizes, own_ref, gate_hbm, up_hbm, down_hbm, out_ref,
+    all_ref, gate_ref, up_ref, down_ref, taken, value, act, part,
+    acc, from_side, from_far, from_mid, from_near, weight_sems,
+    near_sems, mid_sems, far_sems, side_sems, send_sems,
+    back_side_sems, back_far_sems, back_mid_sems, back_near_sems,
+):
+    n0, n1, n2 = sizes
+    count = n0 * n1 * n2
+    rows, width = out_ref.shape
+    inner = gate_ref.shape[1]
+    depth = width // 2
+    group = 2 * n0 * rows
+    loads = [
+        pltpu.make_async_copy(source.at[0], target, weight_sems.at[i])
+        for i, (source, target) in enumerate(
+            ((gate_hbm, gate_ref), (up_hbm, up_ref), (down_hbm, down_ref))
+        )
+    ]
+    for load in loads:
+        load.start()
+    links = Links(sizes)
+    links.barrier()
+
+    def spots(b, c):
+        for s in range(2):
+            base = (links.side if s == 0 else 1 - links.side) * count
+            for j in range(n0):
+                yield (s * n0 + j) * rows, base + links.moved((-j, -b, -c))
+
+    def multiply(half, fixed, first):
+        pairs = [(fixed, i) if half == 0 else (i, fixed) for i in range(2)]
+        for i, (b, c) in enumerate(pairs):
+            for offset, spot in spots(b, c):
+                taken[pl.ds(i * group + offset, rows), :] = all_ref[
+                    spot, :, pl.ds(half * depth, depth)
+                ]
+
+        def column(n, carry):
+            at = pl.ds(pl.multiple_of(n * 256, 256), 256)
+            for which, matrix in enumerate((gate_ref, up_ref)):
+                found = jnp.dot(
+                    taken[...], matrix[pl.ds(half * depth, depth), at],
+                    preferred_element_type=jnp.float32,
+                )
+                for i, (b, c) in enumerate(pairs):
+                    piece = found[i * group : (i + 1) * group]
+                    if not first(b, c):
+                        piece = piece + value[which, b, c, :, at]
+                    value[which, b, c, :, at] = piece
+            return carry
+
+        lax.fori_loop(0, inner // 256, column, 0)
+
+    def halfway(half):
+        if half == 0:
+            loads[0].wait()
+            loads[1].wait()
+            multiply(0, 0, lambda b, c: True)
+        else:
+            multiply(1, 0, lambda b, c: b != 0)
+
+    gather_steps(
+        sizes, links, halfway, own_ref, all_ref, send_sems, near_sems, mid_sems, far_sems, side_sems
+    )
+    multiply(0, 1, lambda b, c: c != 0)
+    multiply(1, 1, lambda b, c: False)
+    loads[2].wait()
+
+    def ready(b):
+        mine = lax.axis_index("dev")
+        for c in range(n2):
+            for offset, spot in spots(b, c):
+                tail = all_ref[spot, :, pl.ds(width, own_ref.shape[1] - width)].astype(jnp.float32)
+                places = lax.broadcasted_iota(jnp.int32, tail.shape, 1)
+                chosen = (places == mine) | (places == mine + count)
+                weight = jnp.sum(jnp.where(chosen, tail, 0.0), axis=1, keepdims=True)
+                gate_val = value[0, b, c, pl.ds(offset, rows), :]
+                up_val = value[1, b, c, pl.ds(offset, rows), :]
+                mixed = gate_val / (1.0 + jnp.exp(-gate_val)) * up_val
+                act[pl.ds(c * group + offset, rows), :] = (mixed * weight).astype(act.dtype)
+
+        def column(n, carry):
+            at = pl.ds(pl.multiple_of(n * 512, 512), 512)
+            found = jnp.dot(act[...], down_ref[:, at], preferred_element_type=jnp.float32)
+            found = found.astype(part.dtype)
+            for c in range(n2):
+                for offset, spot in spots(b, c):
+                    start = c * group + offset
+                    part[spot, :, at] = found[start : start + rows]
+            return carry
+
+        lax.fori_loop(0, width // 512, column, 0)
+
+    sum_steps(
+        sizes, links, ready, part, out_ref, acc, from_side, from_far, from_mid, from_near,
+        send_sems, back_side_sems, back_far_sems, back_mid_sems, back_near_sems,
+    )
+    links.finish()
+
+
+def fused_layer(own, gate_proj, up_proj, down_proj):
+    count = lax.axis_size("dev")
+    sizes = grid_of(count)
+    wide = max(sizes)
+    rows = own.shape[0]
+    _, width, inner = gate_proj.shape
+    slots = sizes[0] * wide
+    group = 2 * sizes[0] * rows
+    kind = own.dtype
+    dma = pltpu.SemaphoreType.DMA
+    return pl.pallas_call(
+        functools.partial(layer_kernel, sizes),
+        out_shape=jax.ShapeDtypeStruct((rows, width), jnp.float32),
+        in_specs=[pl.BlockSpec(memory_space=pltpu.VMEM)]
+        + [pl.BlockSpec(memory_space=pl.ANY)] * 3,
+        out_specs=pl.BlockSpec(memory_space=pltpu.VMEM),
+        scratch_shapes=[
+            pltpu.VMEM((2 * count,) + own.shape, kind),
+            pltpu.VMEM((width, inner), kind),
+            pltpu.VMEM((width, inner), kind),
+            pltpu.VMEM((inner, width), kind),
+            pltpu.VMEM((2 * group, width // 2), kind),
+            pltpu.VMEM((2, 2, 2, group, inner), jnp.float32),
+            pltpu.VMEM((2 * group, inner), kind),
+            pltpu.VMEM((2 * count, rows, width), kind),
+            pltpu.VMEM((count, rows, width), kind),
+            pltpu.VMEM((count, rows, width), kind),
+            pltpu.VMEM((2, slots * wide, rows, width // 2), kind),
+            pltpu.VMEM((2, slots, rows, width // 2), kind),
+            pltpu.VMEM((2, sizes[0], rows, width // 2), kind),
+            dma((3,)),
+            dma((2, wide)),
+            dma((2, slots)),
+            dma((2, slots * wide)),
+            dma((2, count)),
+            dma((4 * (count - 1) + 3 * count,)),
+            dma((count,)),
+            dma((2, slots * wide)),
+            dma((2, slots)),
+            dma((2, sizes[0])),
+        ],
+        compiler_params=pltpu.CompilerParams(
+            collective_id=2, has_side_effects=True, vmem_limit_bytes=VMEM_LIMIT
+        ),
+        name="fused_layer",
+    )(own, gate_proj, up_proj, down_proj)
+
+
 def attend(
     queries,
     cached_key_table,
@@ -393,6 +719,9 @@
     )
     mine = lax.axis_index("dev")
     sent = jnp.concatenate([normed, weight_columns(expert_ids, gate_weights, expert_count)], axis=1)
+    if grid_of(expert_count)[1:] == (2, 2):
+        summed = fused_layer(sent, gate_proj, up_proj, down_proj)
+        return (hidden.astype(jnp.float32) + summed).astype(jnp.bfloat16)
     rows = gather_rows(sent)
     tail = rows[:, width:].astype(jnp.float32)
     places = jnp.arange(tail.shape[1], dtype=jnp.int32)

time: 115 us -> 90 us (0.78)
  matrix products: 28.7 us -> 3.03 us
  Pallas kernels: 76.1 us -> 81.4 us
  local copies, waits for them, and re-layouts: 3.86 us -> 1.28 us
  other arithmetic: 5.81 us -> 3.95 us
    dot_general x2 -> x0, matrix products: 25.7 us -> none  [the longest x1 17 us: on_device(): part = jnp.dot(act, down_proj[0], preferred_element_type=jnp.float32)]
    pallas_call x2 -> x1, Pallas kernels: 76.1 us -> 81.4 us  [fused_layer(): pl.pallas_call(functools.partial(layer_kernel, sizes), out_shape=jax.Shap...]
    unnamed x7 -> x17, local copies, waits for them, and re-layouts: 2.45 us -> 1.25 us
where the time goes in v3:
time: 90 us; the launch traced here: 89.8 us
  Pallas kernels  81.4 us (90%)
  other arithmetic  3.95 us (4%)
  matrix products  3.03 us (3%)
  local copies, waits for them, and re-layouts  1.28 us (1%)
    pallas_call x1, Pallas kernels, fused_layer(): pl.pallas_call(functools.partial(layer_kernel, sizes), out_shape=jax.Shap...  81.4 us
    dot_general x1, matrix products, attend(): jnp.einsum('rkgl,rlkd->rkgd', prob_cached, heads_of_values, preferred_ele...  2.1 us

profile of v3, /device:TPU:0, one launch (start us, length us, event | category | flops | bytes accessed | tf_op | source)
XLA Modules:
  0.0 89.8 jit_solution(12041526143531493787)
XLA Ops:
  0.0 0.0 copy-start
  0.0 0.0 copy-start.2
  0.0 0.0 copy-start.3
  0.0 1.1 %copy.26 = bf16[2,8,32,128]{3,2,1,0:T(8,128)(2,1)S(1)} copy(bf16[2,8,32,128]{3,1,2,0:T(8,128)(2,1)} %bitcast.40) | data formatting | bytes 262144
  1.1 0.7 iota_compare_fusion.1
  1.8 0.0 copy-done
  1.8 0.8 fusion.29
  2.6 0.0 copy-done.2
  2.6 0.2 fusion.30
  2.8 0.3 fusion.15
  3.1 0.0 copy-done.3
  3.2 0.0 copy-start.1
  3.2 0.0 copy-start.4
  3.2 0.0 copy-start.5
  3.2 0.0 copy-start.6
  3.2 2.1 %fusion.12 = f32[16,2,16,128]{3,2,1,0:T(8,128)S(1)} fusion(f32[16,2,16,256]{3,2,1,0:T(8,128)S(1)} %get-tuple-element.12, f32[16,2,16]{2,1,0:T(2,128)S(1)} %get-tuple-element.10, f32[16,2,16]{2,1,0:T(2,128)S(1)} %multiply_maximum_fusion, f32[16,2,128]{2,1,0:T(2,128)S(1)} %reshape.59, f32[16,2,16]{2,1,0:T(2,128)S(1)} %get-tuple-element.9, ...), kind=kOutput, calls=%fused_computation.8 | convolution fusion | flops 34078720 | bytes 2906112 | tf_op jit(solution)/shard_map/rkgl,rlkd->rkgd/dot_general | solution.py:667
  5.3 0.0 copy-done.1
  5.3 0.3 fusion.16
  5.6 0.0 copy-done.4
  5.6 0.1 fusion.18
  5.7 0.0 copy-done.5
  5.7 0.1 copy.20
  5.8 0.0 copy-done.6
  5.8 0.1 copy.21
  5.9 0.1 select_reduce_fusion
  6.0 0.1 fusion.26
  6.1 0.7 pad_maximum_fusion.own_ref
  6.8 81.4 %fused_layer.1 = f32[16,4096]{1,0:T(8,128)} custom-call(bf16[16,4224]{1,0:T(8,128)(2,1)} %pad_maximum_fusion.own_ref, bf16[1,4096,768]{2,1,0:T(8,128)(2,1)} %gate_hbm.1, bf16[1,4096,768]{2,1,0:T(8,128)(2,1)} %up_hbm.1, bf16[1,768,4096]{2,1,0:T(8,128)(2,1)} %down_hbm.1), custom_call_target="tpu_custom_call" | custom-call | tf_op jit(solution)/shard_map/fused_layer/pallas_call | solution.py:590
  88.1 1.6 %fusion.19 = bf16[16,4096]{1,0:T(8,128)(2,1)} fusion(f32[16,4096]{1,0:T(8,128)} %fused_layer.1, bf16[16,4096]{1,0:T(8,128)(2,1)S(1)} %get-tuple-element.6), kind=kLoop, calls=%fused_computation.18 | loop fusion | flops 196608 | bytes 524288 | tf_op jit(solution)/shard_map/convert_element_type | solution.py:724
  (7 shorter events, 0.1 us)
Async XLA Ops:
  0.0 1.8 %copy-start = (bf16[16,256,256]{2,1,0:T(8,128)(2,1)S(1)}, bf16[16,256,256]{2,1,0:T(8,128)(2,1)}, u32[]{:S(2)}) copy-start(bf16[16,256,256]{2,1,0:T(8,128)(2,1)} %param.14) | copy-start | bytes 6291460
  0.0 2.6 %copy-start.2 = (bf16[16,256]{1,0:T(8,128)(2,1)S(1)}, bf16[16,256]{1,0:T(8,128)(2,1)}, u32[]{:S(2)}) copy-start(bf16[16,256]{1,0:T(8,128)(2,1)} %param.16) | copy-start | bytes 24580
  0.0 3.1 %copy-start.3 = (bf16[16,256]{1,0:T(8,128)(2,1)S(1)}, bf16[16,256]{1,0:T(8,128)(2,1)}, u32[]{:S(2)}) copy-start(bf16[16,256]{1,0:T(8,128)(2,1)} %param.17) | copy-start | bytes 24580
  3.2 2.2 %copy-start.1 = (bf16[16,4096]{1,0:T(8,128)(2,1)S(1)}, bf16[16,4096]{1,0:T(8,128)(2,1)}, u32[]{:S(2)}) copy-start(bf16[16,4096]{1,0:T(8,128)(2,1)} %param.19) | copy-start | bytes 393220
  3.2 2.4 %copy-start.4 = (bf16[4096]{0:T(1024)(128)(2,1)S(1)}, bf16[4096]{0:T(1024)(128)(2,1)}, u32[]{:S(2)}) copy-start(bf16[4096]{0:T(1024)(128)(2,1)} %param.20) | copy-start | bytes 24580
  3.2 2.5 %copy-start.5 = (s32[16,8]{0,1:T(8,128)S(1)}, s32[16,8]{0,1:T(8,128)}, u32[]{:S(2)}) copy-start(s32[16,8]{0,1:T(8,128)} %param.21) | copy-start | bytes 1540
  3.2 2.6 %copy-start.6 = (f32[16,8]{0,1:T(8,128)S(1)}, f32[16,8]{0,1:T(8,128)}, u32[]{:S(2)}) copy-start(f32[16,8]{0,1:T(8,128)} %param.22) | copy-start | bytes 1540

commit v4 on v3

--- a/solution.py
+++ b/solution.py
@@ -329,13 +329,19 @@
             )
 
     first, second = (2, 1), (1, 2)
-    for half in range(2):
-        for k in range(1, n0):
+    for k in range(1, n0):
+        for half in range(2):
             links.copy(
                 source((0, 0, 0), half), block((0, 0, 0), half), send_sems,
                 near_sems.at[half, k], links.along(0, k),
             )
-    for j in range(n0):
+    def shifted(j, half, mid, far):
+        steps = [-j, 0, 0]
+        steps[first[half]] = -mid
+        steps[second[half]] = -far
+        return tuple(steps)
+
+    def from_line(j):
         for half in range(2):
             steps = (-j, 0, 0)
             if j:
@@ -344,19 +350,21 @@
             spread(steps, half, second[half], far_sems, j * max(sizes))
             cross(steps, half)
 
-    def shifted(j, half, mid, far):
-        steps = [-j, 0, 0]
-        steps[first[half]] = -mid
-        steps[second[half]] = -far
-        return tuple(steps)
-
-    for j in range(n0):
+    def from_middle(j):
         for half in range(2):
             for k in range(1, sizes[first[half]]):
                 steps = shifted(j, half, k, 0)
                 links.arrived(block(steps, half), send_sems, mid_sems.at[half, j * max(sizes) + k])
                 spread(steps, half, second[half], far_sems, j * max(sizes) + k)
                 cross(steps, half)
+
+    from_line(0)
+    from_middle(0)
+    for j in range(1, n0):
+        from_line(j)
+        if j > 1:
+            from_middle(j - 1)
+    from_middle(n0 - 1)
     all_ref[links.side * count + links.moved((0, 0, 0))] = own_ref[...]
     pending = {(b, c, half) for b in range(n1) for c in range(n2) for half in range(2)}
 
@@ -407,31 +415,41 @@
     def mine(steps):
         return links.moved(steps)
 
-    sent_to = None
-    for i, steps in enumerate(order):
-        if steps[1] != sent_to:
-            sent_to = steps[1]
-            ready(sent_to)
-        links.copy(
-            part_ref.at[(1 - links.side) * count + mine(steps)], from_side.at[i],
-            send_sems, side_sems.at[i], links.other(),
-        )
-
     def total(left, right):
         return (left.astype(jnp.float32) + right.astype(jnp.float32)).astype(jnp.bfloat16)
 
-    for i, steps in enumerate(order):
-        spot = mine(steps)
-        links.arrived(from_side.at[i], send_sems, side_sems.at[i])
-        acc[spot] = total(part_ref[links.side * count + spot], from_side[i])
-        for half in range(2):
-            k = steps[second[half]]
-            if k:
-                slot = (steps[0] * wide + steps[first[half]]) * wide + k
+    def cross(b):
+        for i, steps in enumerate(order):
+            if steps[1] == b:
                 links.copy(
-                    acc.at[spot, :, cuts[half]], from_far.at[half, slot],
-                    send_sems, far_sems.at[half, slot], links.along(second[half], k),
+                    part_ref.at[(1 - links.side) * count + mine(steps)], from_side.at[i],
+                    send_sems, side_sems.at[i], links.other(),
                 )
+
+    def fold(b):
+        for i, steps in enumerate(order):
+            if steps[1] != b:
+                continue
+            spot = mine(steps)
+            links.arrived(from_side.at[i], send_sems, side_sems.at[i])
+            acc[spot] = total(part_ref[links.side * count + spot], from_side[i])
+            for half in range(2):
+                k = steps[second[half]]
+                if k:
+                    slot = (steps[0] * wide + steps[first[half]]) * wide + k
+                    links.copy(
+                        acc.at[spot, :, cuts[half]], from_far.at[half, slot],
+                        send_sems, far_sems.at[half, slot], links.along(second[half], k),
+                    )
+
+    ready(1, 0)
+    ready(1, 1)
+    cross(1)
+    ready(0, 0)
+    fold(1)
+    ready(0, 1)
+    cross(0)
+    fold(0)
 
     def shifted(j, half, mid):
         steps = [j, 0, 0]
@@ -545,9 +563,9 @@
     multiply(1, 1, lambda b, c: False)
     loads[2].wait()
 
-    def ready(b):
+    def ready(b, turn):
         mine = lax.axis_index("dev")
-        for c in range(n2):
+        for c in range(n2 if turn == 0 else 0):
             for offset, spot in spots(b, c):
                 tail = all_ref[spot, :, pl.ds(width, own_ref.shape[1] - width)].astype(jnp.float32)
                 places = lax.broadcasted_iota(jnp.int32, tail.shape, 1)
@@ -568,7 +586,8 @@
                     part[spot, :, at] = found[start : start + rows]
             return carry
 
-        lax.fori_loop(0, width // 512, column, 0)
+        steps = width // 1024
+        lax.fori_loop(turn * steps, (turn + 1) * steps, column, 0)
 
     sum_steps(
         sizes, links, ready, part, out_ref, acc, from_side, from_far, from_mid, from_near,

time: 90 us -> 88.4 us (0.982)
  Pallas kernels: 81.4 us -> 79.8 us
    pallas_call x1, Pallas kernels: 81.4 us -> 79.8 us  [fused_layer(): pl.pallas_call(functools.partial(layer_kernel, sizes), out_shape=jax.Shap...]
where the time goes in v4:
time: 88.4 us; the launch traced here: 88.2 us
  Pallas kernels  79.8 us (90%)
  other arithmetic  3.95 us (4%)
  matrix products  3.03 us (3%)
  local copies, waits for them, and re-layouts  1.28 us (1%)
    pallas_call x1, Pallas kernels, fused_layer(): pl.pallas_call(functools.partial(layer_kernel, sizes), out_shape=jax.Shap...  79.8 us
    dot_general x1, matrix products, attend(): jnp.einsum('rkgl,rlkd->rkgd', prob_cached, heads_of_values, preferred_ele...  2.1 us

profile of v4, /device:TPU:0, one launch (start us, length us, event | category | flops | bytes accessed | tf_op | source)
XLA Modules:
  0.0 88.2 jit_solution(18224140820817857773)
XLA Ops:
  0.0 0.0 copy-start
  0.0 0.0 copy-start.2
  0.0 0.0 copy-start.3
  0.0 1.1 %copy.26 = bf16[2,8,32,128]{3,2,1,0:T(8,128)(2,1)S(1)} copy(bf16[2,8,32,128]{3,1,2,0:T(8,128)(2,1)} %bitcast.40) | data formatting | bytes 262144
  1.1 0.7 iota_compare_fusion.1
  1.8 0.0 copy-done
  1.8 0.8 fusion.29
  2.6 0.0 copy-done.2
  2.6 0.2 fusion.30
  2.8 0.3 fusion.15
  3.1 0.0 copy-done.3
  3.2 0.0 copy-start.1
  3.2 0.0 copy-start.4
  3.2 0.0 copy-start.5
  3.2 0.0 copy-start.6
  3.2 2.1 %fusion.12 = f32[16,2,16,128]{3,2,1,0:T(8,128)S(1)} fusion(f32[16,2,16,256]{3,2,1,0:T(8,128)S(1)} %get-tuple-element.12, f32[16,2,16]{2,1,0:T(2,128)S(1)} %get-tuple-element.10, f32[16,2,16]{2,1,0:T(2,128)S(1)} %multiply_maximum_fusion, f32[16,2,128]{2,1,0:T(2,128)S(1)} %reshape.59, f32[16,2,16]{2,1,0:T(2,128)S(1)} %get-tuple-element.9, ...), kind=kOutput, calls=%fused_computation.8 | convolution fusion | flops 34078720 | bytes 2906112 | tf_op jit(solution)/shard_map/rkgl,rlkd->rkgd/dot_general | solution.py:686
  5.3 0.0 copy-done.1
  5.3 0.3 fusion.16
  5.6 0.0 copy-done.4
  5.6 0.1 fusion.18
  5.7 0.0 copy-done.5
  5.7 0.1 copy.20
  5.8 0.0 copy-done.6
  5.8 0.1 copy.21
  5.9 0.1 select_reduce_fusion
  6.0 0.1 fusion.26
  6.1 0.7 pad_maximum_fusion.own_ref
  6.8 79.8 %fused_layer.1 = f32[16,4096]{1,0:T(8,128)} custom-call(bf16[16,4224]{1,0:T(8,128)(2,1)} %pad_maximum_fusion.own_ref, bf16[1,4096,768]{2,1,0:T(8,128)(2,1)} %gate_hbm.1, bf16[1,4096,768]{2,1,0:T(8,128)(2,1)} %up_hbm.1, bf16[1,768,4096]{2,1,0:T(8,128)(2,1)} %down_hbm.1), custom_call_target="tpu_custom_call" | custom-call | tf_op jit(solution)/shard_map/fused_layer/pallas_call | solution.py:609
  86.5 1.6 %fusion.19 = bf16[16,4096]{1,0:T(8,128)(2,1)} fusion(f32[16,4096]{1,0:T(8,128)} %fused_layer.1, bf16[16,4096]{1,0:T(8,128)(2,1)S(1)} %get-tuple-element.6), kind=kLoop, calls=%fused_computation.18 | loop fusion | flops 196608 | bytes 524288 | tf_op jit(solution)/shard_map/convert_element_type | solution.py:743
  (7 shorter events, 0.1 us)
Async XLA Ops:
  0.0 1.8 %copy-start = (bf16[16,256,256]{2,1,0:T(8,128)(2,1)S(1)}, bf16[16,256,256]{2,1,0:T(8,128)(2,1)}, u32[]{:S(2)}) copy-start(bf16[16,256,256]{2,1,0:T(8,128)(2,1)} %param.14) | copy-start | bytes 6291460
  0.0 2.6 %copy-start.2 = (bf16[16,256]{1,0:T(8,128)(2,1)S(1)}, bf16[16,256]{1,0:T(8,128)(2,1)}, u32[]{:S(2)}) copy-start(bf16[16,256]{1,0:T(8,128)(2,1)} %param.16) | copy-start | bytes 24580
  0.0 3.1 %copy-start.3 = (bf16[16,256]{1,0:T(8,128)(2,1)S(1)}, bf16[16,256]{1,0:T(8,128)(2,1)}, u32[]{:S(2)}) copy-start(bf16[16,256]{1,0:T(8,128)(2,1)} %param.17) | copy-start | bytes 24580
  3.2 2.2 %copy-start.1 = (bf16[16,4096]{1,0:T(8,128)(2,1)S(1)}, bf16[16,4096]{1,0:T(8,128)(2,1)}, u32[]{:S(2)}) copy-start(bf16[16,4096]{1,0:T(8,128)(2,1)} %param.19) | copy-start | bytes 393220
  3.2 2.4 %copy-start.4 = (bf16[4096]{0:T(1024)(128)(2,1)S(1)}, bf16[4096]{0:T(1024)(128)(2,1)}, u32[]{:S(2)}) copy-start(bf16[4096]{0:T(1024)(128)(2,1)} %param.20) | copy-start | bytes 24580
  3.2 2.5 %copy-start.5 = (s32[16,8]{0,1:T(8,128)S(1)}, s32[16,8]{0,1:T(8,128)}, u32[]{:S(2)}) copy-start(s32[16,8]{0,1:T(8,128)} %param.21) | copy-start | bytes 1540
  3.2 2.6 %copy-start.6 = (f32[16,8]{0,1:T(8,128)S(1)}, f32[16,8]{0,1:T(8,128)}, u32[]{:S(2)}) copy-start(f32[16,8]{0,1:T(8,128)} %param.22) | copy-start | bytes 1540
